TPU v7x, 32 devices: a whole 2x2x4 slice. The times are simulated.
32 devices in a mesh: pipe: 4 (over z), tile: 8 (over y, x, core).
Axes of the slice: x: 2, y: 2, z: 4, core: 2. Of those that a mesh axis runs over, the one named last changes fastest.
Arguments:
- x_next: bfloat16 [4, 1024, 8192], P('pipe', 'tile'), may hold values from -6 to 6
- x_saved: bfloat16 [4, 1024, 8192], P('pipe', 'tile'), may hold values from -6 to 6
- pending: bfloat16 [4, 1024, 8192], P('pipe', 'tile'), may hold values from -6 to 6
- gu_rows: int32 [4, 8, 1], P('pipe'), may hold values from 0 to 63, as said below
- gu_cols: int32 [4, 8, 1], P('pipe'), may hold values from 0 to 111
- gu_live: int32 [4, 8], P('pipe'), may hold values from 1 to 1, as said below
- down_rows: int32 [4, 8, 1], P('pipe'), may hold values from 0 to 111, as said below
- down_cols: int32 [4, 8, 1], P('pipe'), may hold values from 0 to 63
- down_live: int32 [4, 8], P('pipe'), may hold values from 1 to 1, as said below
- gate_up_tiles: bfloat16 [4, 8, 1, 2, 128, 128], P('pipe', 'tile'), may hold values from -0.5 to 0.5
- down_tiles: bfloat16 [4, 8, 1, 128, 128], P('pipe', 'tile'), may hold values from -0.5 to 0.5
Outputs:
- y_next: bfloat16 [4, 1024, 8192], P('pipe', 'tile')
- dx_saved: bfloat16 [4, 1024, 8192], P('pipe', 'tile')
- grad_gate_up: float32 [4, 8, 1, 2, 128, 128], P('pipe', 'tile')
- grad_down: float32 [4, 8, 1, 128, 128], P('pipe', 'tile')
Inputs may be any that keep to these rules, and one draw needn't show every extreme that they name: Within a section the 8 x 1 slots of the gate and up lists name distinct tiles (gu_rows, gu_cols). Within a section the 8 x 1 slots of the down list name distinct tiles (down_rows, down_cols). `gu_live`: in every section some owner has all 1 slots live. `down_live`: in every section some owner has all 1 slots live.
All inputs are finite; a program needn't handle non-finite values.
Results may differ from a plain program's by a relative error of at most 0.0067.
Values may be sent and summed in bfloat16 or wider, within the bound.
A program may use at most 128 MiB of HBM per device.

v0:
```python
import jax
import jax.numpy as jnp
from jax import lax
from jax.sharding import PartitionSpec as P


def shifted(value, axis, steps):
    count = lax.axis_size(axis)
    pairs = [(source, (source + steps) % count) for source in range(count)]
    return lax.ppermute(value, axis, pairs)


def sum_columns(received, index, blocks):
    onehot = (index[:, None] == jnp.arange(blocks, dtype=jnp.int32)[None, :]).astype(jnp.bfloat16)
    summed = jnp.einsum("mtsq,sc->mtcq", received, onehot, preferred_element_type=jnp.float32)
    return summed.reshape(summed.shape[0], summed.shape[1], blocks * summed.shape[3])


def match_table(left, right):
    return (left[:, None] == right[None, :]).astype(jnp.bfloat16)


def first_table(g_cols, d_rows):
    count = g_cols.shape[0]
    positions = jnp.arange(count, dtype=jnp.int32)
    earlier = (g_cols[:, None] == g_cols[None, :]) & (positions[None, :] < positions[:, None])
    leading = jnp.logical_not(jnp.any(earlier, axis=1))
    return ((g_cols[:, None] == d_rows[None, :]) & leading[:, None]).astype(jnp.bfloat16)


def slot_sums(received, g_cols):
    return jnp.einsum(
        "mtsq,sk->mtkq", received, match_table(g_cols, g_cols), preferred_element_type=jnp.float32
    )


def pick_hidden(hidden, g_cols, d_rows):
    picked = jnp.einsum(
        "mtkq,kj->mtjq", hidden, first_table(g_cols, d_rows), preferred_element_type=jnp.float32
    )
    return picked.astype(jnp.bfloat16)


def dh_on_slots(dh_parts, d_rows, g_cols):
    return jnp.einsum(
        "tjq,jk->tkq", dh_parts, match_table(d_rows, g_cols), preferred_element_type=jnp.float32
    )


def per_device(
    x_next,
    x_saved,
    pending,
    gu_rows,
    gu_cols,
    gu_live,
    down_rows,
    down_cols,
    down_live,
    gate_up_tiles,
    down_tiles,
):
    owners = lax.axis_size("tile")
    tok_dev = x_next.shape[1]
    width = x_next.shape[2]
    block = down_tiles.shape[-1]
    slots = down_tiles.shape[2]
    row_blocks = width // block
    all_count = owners * slots
    cot = shifted(pending[0], "pipe", -1)
    g_rows = gu_rows[0].reshape(-1)
    g_cols = gu_cols[0].reshape(-1)
    d_rows = down_rows[0].reshape(-1)
    d_cols = down_cols[0].reshape(-1)
    slot_ids = jnp.arange(slots, dtype=jnp.int32)
    both_inputs = jnp.stack([x_next[0], x_saved[0]])
    g_live_all = (slot_ids[None, :] < gu_live[0][:, None]).reshape(all_count).astype(jnp.float32)
    d_live_all = (slot_ids[None, :] < down_live[0][:, None]).reshape(all_count).astype(jnp.float32)
    every_gu, every_down = (
        lax.all_gather(gate_up_tiles[0], "tile", axis=0, tiled=True),
        lax.all_gather(down_tiles[0], "tile", axis=0, tiled=True),
    )
    every_gu = every_gu.reshape(all_count, 2, block, block)
    every_down = every_down.reshape(all_count, block, block)
    x_all = jnp.take(both_inputs.reshape(2, tok_dev, row_blocks, block), g_rows, axis=2)
    parts = jnp.einsum("mtkp,kgpq->mgtkq", x_all, every_gu, preferred_element_type=jnp.float32)
    parts = (parts * g_live_all[:, None]).astype(jnp.bfloat16)
    sums = slot_sums(parts.reshape(4, tok_dev, all_count, block), g_cols).reshape(
        2, 2, tok_dev, all_count, block
    )
    gate = sums[:, 0]
    up = sums[:, 1]
    sig = jax.nn.sigmoid(gate)
    act = gate * sig
    hidden = (act * up).astype(jnp.bfloat16)
    h_all = pick_hidden(hidden, g_cols, d_rows)
    dy_all = jnp.take(cot.reshape(tok_dev, row_blocks, block), d_cols, axis=1)
    y_part = (
        jnp.einsum("tkp,kpq->tkq", h_all[0], every_down, preferred_element_type=jnp.float32)
        * d_live_all[:, None]
    )
    dh_part = (
        jnp.einsum("tkq,kpq->tkp", dy_all, every_down, preferred_element_type=jnp.float32)
        * d_live_all[:, None]
    )
    down_terms = (
        jnp.einsum("tkp,tkq->kpq", h_all[1], dy_all, preferred_element_type=jnp.float32)
        * d_live_all[:, None, None]
    )
    y_out = sum_columns(y_part.astype(jnp.bfloat16)[None], d_cols, row_blocks)[0].astype(
        jnp.bfloat16
    )
    dh = dh_on_slots(dh_part.astype(jnp.bfloat16), d_rows, g_cols)
    d_gate = (dh * up[1] * sig[1] * (1.0 + gate[1] * (1.0 - sig[1]))).astype(jnp.bfloat16)
    d_up = (dh * act[1]).astype(jnp.bfloat16)
    grads_all = jnp.stack([d_gate, d_up])
    gu_terms = jnp.einsum("tkp,gtkq->kgpq", x_all[1], grads_all, preferred_element_type=jnp.float32)
    gu_terms = gu_terms * g_live_all[:, None, None, None]
    dx_part = jnp.einsum("gtkq,kgpq->tkp", grads_all, every_gu, preferred_element_type=jnp.float32)
    dx_part = (dx_part * g_live_all[:, None]).astype(jnp.bfloat16)
    dx_out = sum_columns(dx_part[None], g_rows, row_blocks)[0].astype(jnp.bfloat16)
    grad_gu, grad_down = (
        lax.psum_scatter(
            gu_terms.reshape(owners, slots, 2, block, block),
            "tile",
            scatter_dimension=0,
            tiled=True,
        ),
        lax.psum_scatter(
            down_terms.reshape(owners, slots, block, block), "tile", scatter_dimension=0, tiled=True
        ),
    )
    return (y_out[None], dx_out[None], grad_gu[None], grad_down[None])


def solution(mesh):
    placed = (
        P("pipe", "tile", None),
        P("pipe", "tile", None),
        P("pipe", "tile", None),
        P("pipe", None, None),
        P("pipe", None, None),
        P("pipe", None),
        P("pipe", None, None),
        P("pipe", None, None),
        P("pipe", None),
        P("pipe", "tile", None, None, None, None),
        P("pipe", "tile", None, None, None),
    )
    return jax.shard_map(
        per_device,
        mesh=mesh,
        in_specs=placed,
        out_specs=(
            P("pipe", "tile", None),
            P("pipe", "tile", None),
            P("pipe", "tile", None, None, None, None),
            P("pipe", "tile", None, None, None),
        ),
        check_vma=False,
    )
```

profile of v0, /device:TPU:0, one launch (start us, length us, event | category | flops | bytes accessed | tf_op | source)
XLA Modules:
  0.0 156.9 jit_solution(11414549088401872029)
XLA Ops:
  7.2 0.0 reduce-scatter.3.cloned.1.call-start
  7.2 4.1 %copy.66 = bf16[1,128,8192]{1,2,0:T(8,128)(2,1)} copy(bf16[1,128,8192]{2,1,0:T(8,128)(2,1)} %param.13) | data formatting | bytes 4194304 | tf_op args[2]
  11.3 5.1 %collective-permute-start = (bf16[128,8192]{0,1:T(8,128)(2,1)}, bf16[128,8192]{0,1:T(8,128)(2,1)}, u32[]{:S(2)}, u32[]{:S(2)}) collective-permute-start(bf16[128,8192]{0,1:T(8,128)(2,1)} %bitcast.34), channel_id=1, source_target_pairs={{0,24},{8,0},{16,8},{24,16},{1,25},{9,1},{17,9},{25,17},{2,26},{10... | collective-permute-start | bytes 6291464 | tf_op jit(solution)/shard_map/ppermute | solution.py:10
  16.4 3.2 %copy.56 = bf16[1,128,8192]{1,2,0:T(8,128)(2,1)S(1)} copy(bf16[1,128,8192]{2,1,0:T(8,128)(2,1)} %param.11) | data formatting | bytes 4194304 | tf_op args[0]
  19.6 0.0 copy-start.6
  19.6 0.0 copy-start.2
  19.6 0.0 copy-start.5
  19.6 4.1 %copy.57 = bf16[1,128,8192]{1,2,0:T(8,128)(2,1)} copy(bf16[1,128,8192]{2,1,0:T(8,128)(2,1)} %param.12) | data formatting | bytes 4194304 | tf_op args[1]
  23.7 0.0 copy-done.6
  23.7 0.0 copy-done.2
  23.7 9.9 %all-gather = bf16[8,1,1,2,128,128]{5,4,3,2,1,0:T(8,128)(2,1)S(1)} all-gather(bf16[1,1,1,2,128,128]{5,4,3,2,1,0:T(8,128)(2,1)S(1)} %copy-done.2), channel_id=2, replica_groups=mesh['pipe'=4,'tile'=8] {'tile'}, dimensions={0}, use_global_device_ids=true | all-gather | bytes 589824 | tf_op jit(solution)/shard_map/all_gather | solution.py:80
  33.6 0.0 copy-done.5
  33.6 3.9 %pad_maximum_fusion = bf16[2,128,8192]{1,2,0:T(8,128)(2,1)} fusion(bf16[1,128,8192]{1,2,0:T(8,128)(2,1)} %copy.57, bf16[1,128,8192]{1,2,0:T(8,128)(2,1)S(1)} %copy.56), kind=kLoop, calls=%fused_computation.2 | loop fusion | flops 2097152 | bytes 8388608 | tf_op jit(solution)/shard_map/stack | solution.py:76
  37.5 0.0 copy-start.3
  37.5 0.0 copy-start.8
  37.6 0.0 copy-start.9
  37.6 6.4 %copy.58 = bf16[2,128,64,128]{3,1,2,0:T(8,128)(2,1)} copy(bf16[2,128,64,128]{1,3,2,0:T(8,128)(2,1)} %bitcast.187) | data formatting | bytes 8388608 | tf_op jit(solution)/shard_map/reshape | solution.py:85
  44.0 2.8 %gather_fusion = bf16[8,2,128,128]{3,2,1,0:T(8,128)(2,1)S(1)} fusion(bf16[2,128,64,128]{3,1,2,0:T(8,128)(2,1)} %copy.58, s32[1024]{0:T(1024)S(1)} %pad_clamp_fusion.1), kind=kCustom, calls=%fused_computation | custom fusion | bytes 1048608 | tf_op jit(solution)/shard_map/jit(_take)/gather | solution.py:85
  46.8 0.0 copy-done.3
  46.8 0.0 copy-start.4
  46.8 10.3 %all-gather.1 = bf16[8,1,1,128,128]{4,3,2,1,0:T(8,128)(2,1)} all-gather(bf16[1,1,1,128,128]{4,3,2,1,0:T(8,128)(2,1)S(1)} %copy-done.3), channel_id=3, replica_groups=mesh['pipe'=4,'tile'=8] {'tile'}, dimensions={0}, use_global_device_ids=true | all-gather | bytes 294912 | tf_op jit(solution)/shard_map/all_gather | solution.py:81
  57.1 0.0 copy-done.8
  57.1 0.0 copy-done.9
  57.1 1.0 fusion.39
  58.1 0.4 multiply_convert_fusion
  58.5 0.0 copy-done.4
  58.5 0.7 fusion.12
  59.3 1.6 %add_divide_fusion = (f32[2,128,8,128]{3,2,1,0:T(8,128)}, f32[2,128,8,128]{3,2,1,0:T(8,128)}) fusion(f32[2,2,128,8,128]{4,3,2,1,0:T(8,128)S(1)} %bitcast.188), kind=kLoop, calls=%fused_computation.29 | loop fusion | flops 1048576 | bytes 3145728 | tf_op jit(solution)/shard_map/div | solution.py:93
  60.9 0.7 collective-permute-done
  61.6 0.0 copy-start
  61.6 0.0 copy-start.7
  61.6 4.1 %copy.67 = bf16[128,64,128]{2,0,1:T(8,128)(2,1)} copy(bf16[128,64,128]{0,2,1:T(8,128)(2,1)} %bitcast.35) | data formatting | bytes 4194304 | tf_op jit(solution)/shard_map/reshape | solution.py:97
  65.7 2.2 %gather_fusion.1 = bf16[8,128,128]{2,1,0:T(8,128)(2,1)S(1)} fusion(bf16[128,64,128]{2,0,1:T(8,128)(2,1)} %copy.67, s32[1024]{0:T(1024)S(1)} %pad_clamp_fusion), kind=kCustom, calls=%fused_computation.1 | custom fusion | bytes 524320 | tf_op jit(solution)/shard_map/jit(_take)/gather | solution.py:97
  67.9 0.0 copy-done
  67.9 0.3 fusion.7
  68.2 0.0 copy-done.7
  68.2 1.5 fusion.37
  69.8 0.8 pad_maximum_fusion.1
  70.6 1.4 copy.71
  72.0 2.2 %fusion = f32[8,1,2,128,128]{3,4,2,0,1:T(8,128)} fusion(bf16[2,128,8,128]{1,3,0,2:T(8,128)(2,1)S(1)} %copy.71, f32[8]{0:T(128)S(1)} %fusion.59, bf16[2,128,8,128]{3,1,2,0:T(8,128)(2,1)} %get-tuple-element.22), kind=kOutput, calls=%fused_computation.7 | convolution fusion | flops 67371008 | bytes 1835040 | tf_op jit(solution)/shard_map/tkp,gtkq->kgpq/dot_general | solution.py:117
  74.2 0.0 reduce-scatter.3.cloned.1.call-update
  74.2 0.0 reduce-scatter.5.cloned.1.call-start
  74.3 0.1 fusion.42
  74.4 0.4 fusion.1
  74.8 0.0 copy-start.1
  74.9 1.1 fusion.2
  76.0 0.0 reduce-scatter.5.cloned.1.call-update
  76.0 0.0 copy-done.1
  76.0 0.2 fusion.8
  76.3 0.8 convert_bitcast_fusion.1
  77.1 2.3 %convert_element_type.128 = bf16[1,128,8192]{2,1,0:T(8,128)(2,1)} reshape(bf16[1,128,64,128]{3,2,1,0:T(8,128)(2,1)S(1)} %convert_bitcast_fusion.1) | data formatting | bytes 4194304 | tf_op jit(solution)/shard_map/convert_element_type | solution.py:110
  79.4 0.3 fusion.9
  79.7 0.8 convert_bitcast_fusion
  80.6 2.3 %convert_element_type.138 = bf16[1,128,8192]{2,1,0:T(8,128)(2,1)} reshape(bf16[1,128,64,128]{3,2,1,0:T(8,128)(2,1)S(1)} %convert_bitcast_fusion) | data formatting | bytes 4194304 | tf_op jit(solution)/shard_map/convert_element_type | solution.py:121
  82.9 29.5 %reduce-scatter.3.cloned.1.call-done = f32[1,1,2,128,128]{3,4,2,0,1:T(8,128)} async-done(((f32[8,1,2,128,128]{3,4,2,0,1:T(8,128)}), f32[1,1,2,128,128]{3,4,2,0,1:T(8,128)}) %reduce-scatter.3.cloned.1.call-update) | async-done | bytes 131088 | tf_op jit(solution)/shard_map/reduce_scatter | solution.py:123
  112.3 1.7 %copy.73 = f32[1,1,1,2,128,128]{5,4,3,2,1,0:T(8,128)} copy(f32[1,1,1,2,128,128]{4,5,3,2,1,0:T(8,128)} %bitcast.192) | data formatting | bytes 262144
  114.0 36.1 %reduce-scatter.5.cloned.1.call-done = f32[1,1,128,128]{3,2,0,1:T(8,128)} async-done(((f32[8,1,128,128]{3,2,0,1:T(8,128)}), f32[1,1,128,128]{3,2,0,1:T(8,128)}) %reduce-scatter.5.cloned.1.call-update) | async-done | bytes 65552 | tf_op jit(solution)/shard_map/reduce_scatter | solution.py:129
  (10 shorter events, 0.1 us)
Async XLA Ops:
  7.2 105.2 %reduce-scatter.3.cloned.1.call-start = ((), (), s32[]{:S(2)}) async-start(), calls=%async_computation.2 | async-start | bytes 1179648 | tf_op jit(solution)/shard_map/reduce_scatter | solution.py:123
  11.3 50.3 %collective-permute-start = (bf16[128,8192]{0,1:T(8,128)(2,1)}, bf16[128,8192]{0,1:T(8,128)(2,1)}, u32[]{:S(2)}, u32[]{:S(2)}) collective-permute-start(bf16[128,8192]{0,1:T(8,128)(2,1)} %bitcast.34), channel_id=1, source_target_pairs={{0,24},{8,0},{16,8},{24,16},{1,25},{9,1},{17,9},{25,17},{2,26},{10... | collective-permute-start | bytes 6291464 | tf_op jit(solution)/shard_map/ppermute | solution.py:10
  19.6 4.1 %copy-start.6 = (s32[1,8,1]{1,2,0:T(1,128)S(1)}, s32[1,8,1]{1,2,0:T(1,128)}, u32[]{:S(2)}) copy-start(s32[1,8,1]{1,2,0:T(1,128)} %param.14) | copy-start | bytes 100
  19.6 4.1 %copy-start.2 = (bf16[1,1,1,2,128,128]{5,4,3,2,1,0:T(8,128)(2,1)S(1)}, bf16[1,1,1,2,128,128]{5,4,3,2,1,0:T(8,128)(2,1)}, u32[]{:S(2)}) copy-start(bf16[1,1,1,2,128,128]{5,4,3,2,1,0:T(8,128)(2,1)} %param.20) | copy-start | bytes 196612
  19.6 14.0 %copy-start.5 = (s32[1,8,1]{1,2,0:T(1,128)S(1)}, s32[1,8,1]{1,2,0:T(1,128)}, u32[]{:S(2)}) copy-start(s32[1,8,1]{1,2,0:T(1,128)} %param.18) | copy-start | bytes 100
  37.5 9.3 %copy-start.3 = (bf16[1,1,1,128,128]{4,3,2,1,0:T(8,128)(2,1)S(1)}, bf16[1,1,1,128,128]{4,3,2,1,0:T(8,128)(2,1)}, u32[]{:S(2)}) copy-start(bf16[1,1,1,128,128]{4,3,2,1,0:T(8,128)(2,1)} %param.21) | copy-start | bytes 98308
  37.5 19.5 %copy-start.8 = (s32[1,8]{1,0:T(1,128)S(1)}, s32[1,8]{1,0:T(1,128)}, u32[]{:S(2)}) copy-start(s32[1,8]{1,0:T(1,128)} %param.16) | copy-start | bytes 100
  37.6 19.6 %copy-start.9 = (s32[1,8]{1,0:T(1,128)S(1)}, s32[1,8]{1,0:T(1,128)}, u32[]{:S(2)}) copy-start(s32[1,8]{1,0:T(1,128)} %param.19) | copy-start | bytes 100
  46.8 11.7 %copy-start.4 = (s32[1,8,1]{1,2,0:T(1,128)S(1)}, s32[1,8,1]{1,2,0:T(1,128)}, u32[]{:S(2)}) copy-start(s32[1,8,1]{1,2,0:T(1,128)} %param.15) | copy-start | bytes 100
  61.6 6.3 %copy-start = (bf16[8,1,1,128,128]{4,3,2,1,0:T(8,128)(2,1)S(1)}, bf16[8,1,1,128,128]{4,3,2,1,0:T(8,128)(2,1)}, u32[]{:S(2)}) copy-start(bf16[8,1,1,128,128]{4,3,2,1,0:T(8,128)(2,1)} %all-gather.1) | copy-start | bytes 786436
  61.6 6.7 %copy-start.7 = (s32[1,8,1]{1,2,0:T(1,128)S(1)}, s32[1,8,1]{1,2,0:T(1,128)}, u32[]{:S(2)}) copy-start(s32[1,8,1]{1,2,0:T(1,128)} %param.17) | copy-start | bytes 100
  74.2 75.9 %reduce-scatter.5.cloned.1.call-start = ((), (), s32[]{:S(2)}) async-start(), calls=%async_computation.3 | async-start | bytes 589824 | tf_op jit(solution)/shard_map/reduce_scatter | solution.py:129
  74.8 1.2 copy-start.1
Sparse Core Ops, SparseCore 0:
  74.4 37.9 reduce-scatter.2
  116.0 34.0 reduce-scatter.4
where the time goes:
time: 158 us; the launch traced here: 157 us
  waiting for transfers between devices  66.3 us (42%)
  local copies, waits for them, and re-layouts  34.6 us (22%)
  blocking collectives  20.1 us (13%)
  between operations  14.3 us (9%)
  matrix products  9.02 us (6%)
  other arithmetic  7.47 us (5%)
  starting transfers between devices  5.16 us (3%)
    reduce_scatter x1, waiting for transfers between devices, per_device(): lax.psum_scatter(down_terms.reshape(owners, slots, block, block), 'tile',...  36.1 us
    reduce_scatter x1, waiting for transfers between devices, per_device(): lax.psum_scatter(gu_terms.reshape(owners, slots, 2, block, block), 'tile'...  29.5 us
    unnamed x24, local copies, waits for them, and re-layouts  13.1 us
    all_gather x1, blocking collectives, per_device(): lax.all_gather(down_tiles[0], 'tile', axis=0, tiled=True)  10.3 us
    all_gather x1, blocking collectives, per_device(): lax.all_gather(gate_up_tiles[0], 'tile', axis=0, tiled=True)  9.86 us
    reshape x1, local copies, waits for them, and re-layouts, per_device(): both_inputs.reshape(2, tok_dev, row_blocks, block)  6.38 us
    ppermute x1, starting transfers between devices, shifted(): return lax.ppermute(value, axis, pairs)  5.08 us
    reshape x1, local copies, waits for them, and re-layouts, per_device(): dy_all = jnp.take(cot.reshape(tok_dev, row_blocks, block), d_cols, axis=1)  4.1 us
  transfers between devices with their start and end apart: 3, of which 3 were waited for; matrix products, arithmetic and copies ran while one was open for 22% of the time, Pallas kernels for 0%

commit v1 on v0

v1 whole, which is shorter than its diff:
```python
import functools
import math

import jax
import jax.numpy as jnp
from jax import lax
from jax.experimental import pallas as pl
from jax.experimental.pallas import tpu as pltpu
from jax.sharding import PartitionSpec as P

F32 = jnp.float32
BF16 = jnp.bfloat16
I32 = jnp.int32


def dot(a, b, ca, cb):
    return lax.dot_general(a, b, (((ca,), (cb,)), ((), ())), preferred_element_type=F32)


def loop(count, body):
    def step(i, carry):
        body(i)
        return carry

    lax.fori_loop(0, count, step, 0)


def relay_kernel(
    n,
    pipes,
    side,
    g_rows,
    g_cols,
    g_live,
    d_rows,
    d_cols,
    d_live,
    gu_ref,
    dn_ref,
    xn_hbm,
    xs_hbm,
    pd_hbm,
    y_ref,
    dx_ref,
    ggu_ref,
    gdn_ref,
    xn,
    xs,
    pd,
    idx,
    gu_all,
    dn_all,
    cot_out,
    cot,
    xb,
    gate,
    up,
    hid,
    dh,
    dg,
    gu_give,
    gu_got,
    gu_own,
    gu_out,
    gu_in,
    dn_give,
    dn_got,
    dn_own,
    dn_out,
    dn_in,
    local_sem,
    idx_sem,
    gu_send,
    gu_recv,
    dn_send,
    dn_recv,
    cot_send,
    cot_recv,
    half_send,
    half_recv,
    full_send,
    full_recv,
):
    chips = n // 2
    tok = xn.shape[1]
    blk = dn_ref.shape[-1]
    me = lax.axis_index("tile")
    stage = lax.axis_index("pipe")
    core = me % 2
    chip = me // 2
    partner = chip * 2 + 1 - core
    chip_y, chip_x = chip // side, chip % side
    rows_of_chips = chips // side
    offsets = [(dy, dx) for dy in range(rows_of_chips) for dx in range(side)]
    offsets = sorted(offsets[1:], key=lambda o: -(o[0] + o[1]))
    peer_chips = [
        ((chip_y + dy) % rows_of_chips) * side + (chip_x + dx) % side for dy, dx in offsets
    ]
    peers = [c * 2 + core for c in peer_chips]
    nxt, prv = (stage + 1) % pipes, (stage + pipes - 1) % pipes

    def remote(src, dst, send, recv, **where):
        return pltpu.make_async_remote_copy(
            src_ref=src, dst_ref=dst, send_sem=send, recv_sem=recv, device_id=where
        )

    def fetch(hbm, buf, at):
        def piece(b):
            cols = pl.ds(pl.multiple_of(b * blk, blk), blk)
            pltpu.make_async_copy(hbm.at[:, cols], buf.at[b], local_sem.at[at]).start()

        loop(buf.shape[0], piece)

    barrier = pltpu.get_barrier_semaphore()
    for where in (nxt, prv):
        pl.semaphore_signal(barrier, inc=1, device_id={"pipe": where})
    for peer in peers + [partner]:
        pl.semaphore_signal(barrier, inc=1, device_id={"tile": peer})
    fetch(pd_hbm, pd, 0)
    pl.semaphore_wait(barrier, len(peers) + 3)

    idx_copy = remote(d_cols, idx, idx_sem.at[0], idx_sem.at[1], pipe=nxt)
    idx_copy.start()
    sends = []

    def start(copy):
        copy.start()
        sends.append(copy)

    for i, peer in enumerate(peers + [partner]):
        start(remote(gu_ref, gu_all.at[me], gu_send.at[i], gu_recv.at[me], tile=peer))
    for i, peer in enumerate(peers + [partner]):
        start(remote(dn_ref, dn_all.at[me], dn_send.at[i], dn_recv.at[me], tile=peer))
    fetch(xs_hbm, xs, 1)
    fetch(xn_hbm, xn, 2)
    gu_all[me] = gu_ref[...]
    dn_all[me] = dn_ref[...]

    order = [2 * c + 1 - core for c in range(chips)] + [2 * c + core for c in range(chips)]

    idx_copy.wait_recv()
    pltpu.make_async_copy(pd, pd, local_sem.at[0]).wait()
    for slot in order:
        cot_out[slot] = pd[idx[0, slot, 0]]
        start(
            remote(
                cot_out.at[slot], cot.at[slot], cot_send.at[slot], cot_recv.at[slot], pipe=prv
            )
        )

    pltpu.make_async_copy(xs, xs, local_sem.at[1]).wait()
    pltpu.make_async_copy(xn, xn, local_sem.at[2]).wait()

    def fill(k):
        row = g_rows[0, k, 0]
        xb[k, :tok] = xn[row]
        xb[k, tok:] = xs[row]

    loop(n, fill)
    hid[n] = jnp.zeros((2 * tok, blk), BF16)

    def project(j, first):
        live = (g_live[0, j] > 0).astype(F32)
        for g, acc in ((0, gate), (1, up)):
            part = (dot(xb[j], gu_all[j, g], 1, 0) * live).astype(BF16).astype(F32)

            def add(k):
                same = (g_cols[0, j, 0] == g_cols[0, k, 0]).astype(F32)
                if first:
                    acc[k] = part * same
                else:
                    acc[k] = acc[k] + part * same

            loop(n, add)

    def gu_arrival(o):
        remote(gu_ref, gu_all.at[o], gu_send.at[0], gu_recv.at[o], tile=partner).wait_recv()

    def dn_arrival(o):
        remote(dn_ref, dn_all.at[o], dn_send.at[0], dn_recv.at[o], tile=partner).wait_recv()

    project(me, True)
    gu_arrival(partner)
    project(partner, False)
    for i, peer in enumerate(peers):
        gu_arrival(peer)
        start(
            remote(
                gu_all.at[peer], gu_all.at[peer], gu_send.at[chips + i], gu_recv.at[peer],
                tile=partner,
            )
        )
        project(peer, False)
    for i, peer in enumerate(peers):
        dn_arrival(peer)
        start(
            remote(
                dn_all.at[peer], dn_all.at[peer], dn_send.at[chips + i], dn_recv.at[peer],
                tile=partner,
            )
        )
    for c in peer_chips:
        other = c * 2 + 1 - core
        gu_arrival(other)
        project(other, False)

    def activate(k):
        gn = gate[k, :tok]
        hid[k, :tok] = (gn * jax.nn.sigmoid(gn) * up[k, :tok]).astype(BF16)
        g = gate[k, tok:]
        u = up[k, tok:]
        sig = jax.nn.sigmoid(g)
        act = g * sig
        hid[k, tok:] = (act * u).astype(BF16)
        gate[k, tok:] = u * sig * (1.0 + g * (1.0 - sig))
        up[k, tok:] = act

    loop(n, activate)

    def hidden_slot(j):
        found = jnp.int32(n)
        for k in range(n):
            back = n - 1 - k
            same = (g_cols[0, back, 0] == d_rows[0, j, 0]).astype(I32)
            found = found + same * (back - found)
        return found

    dn_arrival(partner)
    for c in peer_chips:
        dn_arrival(c * 2 + 1 - core)

    def forward(j):
        live = (d_live[0, j] > 0).astype(F32)
        h = hid[hidden_slot(j), :tok]
        y_ref[j] = (dot(h, dn_all[j], 1, 0) * live).astype(BF16)

    loop(n, forward)

    def zero(k):
        dh[k] = jnp.zeros((tok, blk), F32)

    loop(n, zero)

    for at, slot in enumerate(order):
        c = at % chips
        live = (d_live[0, slot] > 0).astype(F32)
        remote(
            cot_out.at[slot], cot.at[slot], cot_send.at[slot], cot_recv.at[slot], pipe=nxt
        ).wait_recv()
        dy = cot[slot]
        part = (dot(dy, dn_all[slot], 1, 1) * live).astype(BF16).astype(F32)

        def add(k):
            same = (d_rows[0, slot, 0] == g_cols[0, k, 0]).astype(F32)
            dh[k] = dh[k] + part * same

        loop(n, add)
        term = dot(hid[hidden_slot(slot), tok:], dy, 0, 0) * live
        if at < chips:
            dn_give[c] = term.astype(BF16)
            start(
                remote(
                    dn_give.at[c], dn_got.at[c], half_send.at[0, c], half_recv.at[0, c],
                    tile=partner,
                )
            )
        else:
            dn_own[c] = term

    def grads(k):
        d = dh[k]
        dg[k, 0] = (d * gate[k, tok:]).astype(BF16)
        dg[k, 1] = (d * up[k, tok:]).astype(BF16)

    loop(n, grads)

    def gu_term(slot, g):
        live = (g_live[0, slot] > 0).astype(F32)
        return dot(xb[slot, tok:], dg[slot, g], 0, 0) * live

    for c in range(chips):
        slot = 2 * c + 1 - core
        for g in range(2):
            gu_give[c, g] = gu_term(slot, g).astype(BF16)
        start(
            remote(
                gu_give.at[c], gu_got.at[c], half_send.at[1, c], half_recv.at[1, c], tile=partner
            )
        )

    def half_arrival(kind, give, got, c):
        remote(
            give.at[c], got.at[c], half_send.at[kind, c], half_recv.at[kind, c], tile=partner
        ).wait_recv()

    for i, c in enumerate(peer_chips):
        half_arrival(0, dn_give, dn_got, c)
        dn_out[i] = (dn_own[c] + dn_got[c].astype(F32)).astype(BF16)
        start(
            remote(
                dn_out.at[i], dn_in.at[chip], full_send.at[0, i], full_recv.at[0, chip],
                tile=2 * c + core,
            )
        )
    for c in range(chips):
        for g in range(2):
            gu_own[c, g] = gu_term(2 * c + core, g)
    for i, c in enumerate(peer_chips):
        half_arrival(1, gu_give, gu_got, c)
        for g in range(2):
            gu_out[i, g] = (gu_own[c, g] + gu_got[c, g].astype(F32)).astype(BF16)
        start(
            remote(
                gu_out.at[i], gu_in.at[chip], full_send.at[1, i], full_recv.at[1, chip],
                tile=2 * c + core,
            )
        )

    def backward(k):
        live = (g_live[0, k] > 0).astype(F32)
        both = dot(dg[k, 0], gu_all[k, 0], 1, 1) + dot(dg[k, 1], gu_all[k, 1], 1, 1)
        dx_ref[k] = (both * live).astype(BF16)

    loop(n, backward)

    half_arrival(0, dn_give, dn_got, chip)
    half_arrival(1, gu_give, gu_got, chip)
    total_dn = dn_own[chip] + dn_got[chip].astype(F32)
    for c in peer_chips:
        remote(
            dn_out.at[0], dn_in.at[c], full_send.at[0, 0], full_recv.at[0, c], tile=partner
        ).wait_recv()
        total_dn = total_dn + dn_in[c].astype(F32)
    gdn_ref[...] = total_dn
    for c in peer_chips:
        remote(
            gu_out.at[0], gu_in.at[c], full_send.at[1, 0], full_recv.at[1, c], tile=partner
        ).wait_recv()
    for g in range(2):
        total = gu_own[chip, g] + gu_got[chip, g].astype(F32)
        for c in peer_chips:
            total = total + gu_in[c, g].astype(F32)
        ggu_ref[g] = total
    idx_copy.wait_send()
    for copy in sends:
        copy.wait_send()


def place_kernel(n, d_cols, g_rows, y_part, dx_part, y_hbm, dx_hbm, y_buf, dx_buf, sem):
    tok, blk = y_part.shape[1:]
    copies = []
    for at, (index, part, buf, hbm) in enumerate(
        ((d_cols, y_part, y_buf, y_hbm), (g_rows, dx_part, dx_buf, dx_hbm))
    ):
        buf[...] = jnp.zeros_like(buf)

        def put(j):
            def add(k, total):
                same = (index[0, k, 0] == index[0, j, 0]).astype(F32)
                return total + part[k].astype(F32) * same

            total = lax.fori_loop(0, n, add, jnp.zeros((tok, blk), F32))
            col = pl.multiple_of(index[0, j, 0] * blk, blk)
            buf[:, pl.ds(col, blk)] = total.astype(BF16)

        loop(n, put)
        copy = pltpu.make_async_copy(buf, hbm, sem.at[at])
        copy.start()
        copies.append(copy)
    for copy in copies:
        copy.wait()


def per_device(
    pipes,
    n,
    x_next,
    x_saved,
    pending,
    gu_rows,
    gu_cols,
    gu_live,
    down_rows,
    down_cols,
    down_live,
    gate_up_tiles,
    down_tiles,
):
    tok, width = x_next.shape[1:]
    blk = down_tiles.shape[-1]
    chips = n // 2
    side = math.isqrt(chips)
    if side * side != chips:
        side = 1
    smem = pl.BlockSpec(memory_space=pltpu.SMEM)
    vmem = pl.BlockSpec(memory_space=pltpu.VMEM)
    hbm = pl.BlockSpec(memory_space=pl.ANY)
    dma = pltpu.SemaphoreType.DMA
    y_part, dx_part, ggu, gdn = pl.pallas_call(
        functools.partial(relay_kernel, n, pipes, side),
        name="relay",
        out_shape=(
            jax.ShapeDtypeStruct((n, tok, blk), BF16),
            jax.ShapeDtypeStruct((n, tok, blk), BF16),
            jax.ShapeDtypeStruct((2, blk, blk), F32),
            jax.ShapeDtypeStruct((blk, blk), F32),
        ),
        in_specs=[smem] * 6 + [vmem] * 2 + [hbm] * 3,
        out_specs=(vmem, vmem, vmem, vmem),
        scratch_shapes=[
            pltpu.VMEM((width // blk, tok, blk), BF16),
            pltpu.VMEM((width // blk, tok, blk), BF16),
            pltpu.VMEM((width // blk, tok, blk), BF16),
            pltpu.SMEM((1, n, 1), I32),
            pltpu.VMEM((n, 2, blk, blk), BF16),
            pltpu.VMEM((n, blk, blk), BF16),
            pltpu.VMEM((n, tok, blk), BF16),
            pltpu.VMEM((n, tok, blk), BF16),
            pltpu.VMEM((n, 2 * tok, blk), BF16),
            pltpu.VMEM((n, 2 * tok, blk), F32),
            pltpu.VMEM((n, 2 * tok, blk), F32),
            pltpu.VMEM((n + 1, 2 * tok, blk), BF16),
            pltpu.VMEM((n, tok, blk), F32),
            pltpu.VMEM((n, 2, tok, blk), BF16),
            pltpu.VMEM((chips, 2, blk, blk), BF16),
            pltpu.VMEM((chips, 2, blk, blk), BF16),
            pltpu.VMEM((chips, 2, blk, blk), F32),
            pltpu.VMEM((chips, 2, blk, blk), BF16),
            pltpu.VMEM((chips, 2, blk, blk), BF16),
            pltpu.VMEM((chips, blk, blk), BF16),
            pltpu.VMEM((chips, blk, blk), BF16),
            pltpu.VMEM((chips, blk, blk), F32),
            pltpu.VMEM((chips, blk, blk), BF16),
            pltpu.VMEM((chips, blk, blk), BF16),
            dma((3,)),
            dma((2,)),
            dma((2 * chips,)),
            dma((n,)),
            dma((2 * chips,)),
            dma((n,)),
            dma((n,)),
            dma((n,)),
            dma((2, chips)),
            dma((2, chips)),
            dma((2, chips)),
            dma((2, chips)),
        ],
        compiler_params=pltpu.CompilerParams(
            collective_id=0, has_side_effects=True, vmem_limit_bytes=60 * 1024 * 1024
        ),
    )(
        gu_rows,
        gu_cols,
        gu_live,
        down_rows,
        down_cols,
        down_live,
        gate_up_tiles.reshape(2, blk, blk),
        down_tiles.reshape(blk, blk),
        x_next.reshape(tok, width),
        x_saved.reshape(tok, width),
        pending.reshape(tok, width),
    )
    y, dx = pl.pallas_call(
        functools.partial(place_kernel, n),
        name="place",
        out_shape=(
            jax.ShapeDtypeStruct((tok, width), BF16),
            jax.ShapeDtypeStruct((tok, width), BF16),
        ),
        in_specs=[smem] * 2 + [vmem] * 2,
        out_specs=(hbm, hbm),
        scratch_shapes=[
            pltpu.VMEM((tok, width), BF16),
            pltpu.VMEM((tok, width), BF16),
            dma((2,)),
        ],
        compiler_params=pltpu.CompilerParams(vmem_limit_bytes=32 * 1024 * 1024),
    )(down_cols, gu_rows, y_part, dx_part)
    return (
        y[None],
        dx[None],
        ggu.reshape(1, 1, 1, 2, blk, blk),
        gdn.reshape(1, 1, 1, blk, blk),
    )


def solution(mesh):
    tokens = P("pipe", "tile", None)
    lists = P("pipe", None, None)
    lives = P("pipe", None)
    gu_place = P("pipe", "tile", None, None, None, None)
    dn_place = P("pipe", "tile", None, None, None)
    return jax.shard_map(
        functools.partial(per_device, mesh.shape["pipe"], mesh.shape["tile"]),
        mesh=mesh,
        in_specs=(
            tokens, tokens, tokens, lists, lists, lives, lists, lists, lives, gu_place, dn_place,
        ),
        out_specs=(tokens, tokens, gu_place, dn_place),
        check_vma=False,
    )
```

time: 158 us -> 45.3 us (0.29)
  waiting for transfers between devices: 66.3 us -> 0 us
  Pallas kernels: 0 us -> 33.9 us
  local copies, waits for them, and re-layouts: 34.6 us -> 10.2 us
  blocking collectives: 20.1 us -> 0 us
  between operations: 14.3 us -> 0.68 us
  matrix products: 9.02 us -> 0 us
  other arithmetic: 7.47 us -> 0 us
  starting transfers between devices: 5.16 us -> 0 us
    reduce_scatter x2 -> x0, waiting for transfers between devices: 65.6 us -> none  [the longest x1 36.1 us: per_device(): lax.psum_scatter(down_terms.reshape(owners, slots, block, block), 'tile',...]
    pallas_call x0 -> x2, Pallas kernels: none -> 33.9 us  [the longest x1 29.7 us: per_device(): pl.pallas_call(functools.partial(relay_kernel, n, pipes, side), name='rel...]
    all_gather x2 -> x0, blocking collectives: 20.1 us -> none  [the longest x1 10.3 us: per_device(): lax.all_gather(down_tiles[0], 'tile', axis=0, tiled=True)]
    reshape x2 -> x0, local copies, waits for them, and re-layouts: 10.5 us -> none  [the longest x1 6.38 us: per_device(): both_inputs.reshape(2, tok_dev, row_blocks, block)]
    dot_general x11 -> x0, matrix products: 9.02 us -> none  [the longest x1 2.21 us: per_device(): jnp.einsum('tkp,gtkq->kgpq', x_all[1], grads_all, preferred_element_type=...]
    ppermute x1 -> x0, starting transfers between devices: 5.08 us -> none  [shifted(): return lax.ppermute(value, axis, pairs)]
    gather x2 -> x0, local copies, waits for them, and re-layouts: 5.02 us -> none  [the longest x1 2.83 us: per_device(): jnp.take(both_inputs.reshape(2, tok_dev, row_blocks, block), g_rows, axis=2)]
    another operation x2 -> x0, other arithmetic: 4.77 us -> none  [the longest x1 3.92 us: per_device(): both_inputs = jnp.stack([x_next[0], x_saved[0]])]
  transfers between devices with their start and end apart: 3 -> 0, of which waited for: 3 -> 0; matrix products, arithmetic and copies ran while one was open for 22% -> 0% of each run, Pallas kernels for 0% -> 0%
where the time goes in v1:
time: 45.3 us; the launch traced here: 44.8 us
  Pallas kernels  33.9 us (75%)
  local copies, waits for them, and re-layouts  10.2 us (23%)
  between operations  0.68 us (2%)
    pallas_call x1, Pallas kernels, per_device(): pl.pallas_call(functools.partial(relay_kernel, n, pipes, side), name='rel...  29.7 us
    unnamed x14, local copies, waits for them, and re-layouts  10.2 us
    pallas_call x1, Pallas kernels, per_device(): pl.pallas_call(functools.partial(place_kernel, n), name='place', out_shap...  4.28 us

profile of v1, /device:TPU:0, one launch (start us, length us, event | category | flops | bytes accessed | tf_op | source)
XLA Modules:
  0.0 44.8 jit_solution(11204472877492405673)
XLA Ops:
  0.6 1.3 %copy.20.g_rows = s32[1,8,1]{2,1,0:T(8,128)} copy(s32[1,8,1]{1,2,0:T(1,128)} %param.14) | data formatting | bytes 64 | tf_op args[3]
  2.0 1.3 %copy.19.d_cols = s32[1,8,1]{2,1,0:T(8,128)} copy(s32[1,8,1]{1,2,0:T(1,128)} %param.18) | data formatting | bytes 64 | tf_op args[7]
  3.3 1.3 %copy.16.g_cols = s32[1,8,1]{2,1,0:T(8,128)} copy(s32[1,8,1]{1,2,0:T(1,128)} %param.15) | data formatting | bytes 64 | tf_op args[4]
  4.6 1.3 %copy.17.d_rows = s32[1,8,1]{2,1,0:T(8,128)} copy(s32[1,8,1]{1,2,0:T(1,128)} %param.17) | data formatting | bytes 64 | tf_op args[6]
  5.9 0.0 copy-start.2
  5.9 0.0 copy-start.3
  5.9 29.7 %relay.1 = (bf16[8,128,128]{2,1,0:T(8,128)(2,1)}, bf16[8,128,128]{2,1,0:T(8,128)(2,1)}, f32[2,128,128]{2,1,0:T(8,128)}, f32[128,128]{1,0:T(8,128)}) custom-call(s32[1,8,1]{2,1,0:T(8,128)} %copy.20.g_rows, s32[1,8,1]{2,1,0:T(8,128)} %copy.16.g_cols, s32[1,8]{1,0:T(1,128)} %g_live.1, s32[1,8,1]{2,1,0:T(8,128)} %copy.17.d_rows, s32[1,8,1]{2,1,0:T(8,128)} %copy.19.d_cols, ...), custom_call_target="tpu_custom_call" | custom-call | tf_op jit(solution)/shard_map/relay/pallas_call | solution.py:399
  35.6 0.0 copy-done.2
  35.6 0.0 copy-done.3
  35.6 0.0 copy-start
  35.6 0.9 %copy-done = bf16[8,128,128]{2,1,0:T(8,128)(2,1)S(1)} copy-done((bf16[8,128,128]{2,1,0:T(8,128)(2,1)S(1)}, bf16[8,128,128]{2,1,0:T(8,128)(2,1)}, u32[]{:S(2)}) %copy-start) | copy-done | bytes 262168
  36.6 0.0 copy-start.1
  36.6 0.9 %copy-done.1 = bf16[8,128,128]{2,1,0:T(8,128)(2,1)S(1)} copy-done((bf16[8,128,128]{2,1,0:T(8,128)(2,1)S(1)}, bf16[8,128,128]{2,1,0:T(8,128)(2,1)}, u32[]{:S(2)}) %copy-start.1) | copy-done | bytes 262168
  37.5 4.3 %place.1 = (bf16[128,8192]{1,0:T(8,128)(2,1)}, bf16[128,8192]{1,0:T(8,128)(2,1)}) custom-call(s32[1,8,1]{2,1,0:T(8,128)S(1)} %copy-done.3, s32[1,8,1]{2,1,0:T(8,128)S(1)} %copy-done.2, bf16[8,128,128]{2,1,0:T(8,128)(2,1)S(1)} %copy-done, bf16[8,128,128]{2,1,0:T(8,128)(2,1)S(1)} %copy-done.1), custom_call_target="tpu_custom_call" | custom-call | tf_op jit(solution)/shard_map/place/pallas_call | solution.py:464
  41.8 1.6 %copy.23 = f32[1,1,1,2,128,128]{5,4,3,2,1,0:T(8,128)} copy(f32[1,1,1,2,128,128]{5,4,3,2,1,0:T(8,128)} %bitcast.12) | data formatting | bytes 262144
  43.4 1.5 %copy.24 = f32[1,1,1,128,128]{4,3,2,1,0:T(8,128)} copy(f32[1,1,1,128,128]{4,3,2,1,0:T(8,128)} %bitcast.14) | data formatting | bytes 131072
Async XLA Ops:
  5.9 29.7 %copy-start.2 = (s32[1,8,1]{2,1,0:T(8,128)S(1)}, s32[1,8,1]{2,1,0:T(8,128)}, u32[]{:S(2)}) copy-start(s32[1,8,1]{2,1,0:T(8,128)} %copy.20.g_rows) | copy-start | bytes 100
  5.9 29.7 %copy-start.3 = (s32[1,8,1]{2,1,0:T(8,128)S(1)}, s32[1,8,1]{2,1,0:T(8,128)}, u32[]{:S(2)}) copy-start(s32[1,8,1]{2,1,0:T(8,128)} %copy.19.d_cols) | copy-start | bytes 100
  35.6 1.0 %copy-start = (bf16[8,128,128]{2,1,0:T(8,128)(2,1)S(1)}, bf16[8,128,128]{2,1,0:T(8,128)(2,1)}, u32[]{:S(2)}) copy-start(bf16[8,128,128]{2,1,0:T(8,128)(2,1)} %get-tuple-element.10.y_part) | copy-start | bytes 786436
  36.6 0.9 %copy-start.1 = (bf16[8,128,128]{2,1,0:T(8,128)(2,1)S(1)}, bf16[8,128,128]{2,1,0:T(8,128)(2,1)}, u32[]{:S(2)}) copy-start(bf16[8,128,128]{2,1,0:T(8,128)(2,1)} %get-tuple-element.11.dx_part) | copy-start | bytes 786436

commit v2 on v1

--- a/solution.py
+++ b/solution.py
@@ -23,6 +23,22 @@
         return carry
 
     lax.fori_loop(0, count, step, 0)
+
+
+def each(count, body):
+    if count <= 8:
+        for i in range(count):
+            body(i)
+    else:
+        loop(count, body)
+
+
+def latest(keys, key, count, none):
+    found = jnp.int32(none)
+    for q in range(count):
+        same = (keys[q] == key).astype(I32)
+        found = found + same * (q - found)
+    return found
 
 
 def relay_kernel(
@@ -55,8 +71,11 @@
     xb,
     gate,
     up,
+    slope,
     hid,
     dh,
+    y_sum,
+    dx_sum,
     dg,
     gu_give,
     gu_got,
@@ -133,15 +152,19 @@
         start(remote(dn_ref, dn_all.at[me], dn_send.at[i], dn_recv.at[me], tile=peer))
     fetch(xs_hbm, xs, 1)
     fetch(xn_hbm, xn, 2)
-    gu_all[me] = gu_ref[...]
-    dn_all[me] = dn_ref[...]
+    own_tiles = [
+        pltpu.make_async_copy(gu_ref, gu_all.at[me], local_sem.at[3]),
+        pltpu.make_async_copy(dn_ref, dn_all.at[me], local_sem.at[4]),
+    ]
+    for copy in own_tiles:
+        copy.start()
 
     order = [2 * c + 1 - core for c in range(chips)] + [2 * c + core for c in range(chips)]
 
     idx_copy.wait_recv()
     pltpu.make_async_copy(pd, pd, local_sem.at[0]).wait()
     for slot in order:
-        cot_out[slot] = pd[idx[0, slot, 0]]
+        cot_out[slot] = pd[idx[0, slot]]
         start(
             remote(
                 cot_out.at[slot], cot.at[slot], cot_send.at[slot], cot_recv.at[slot], pipe=prv
@@ -152,26 +175,31 @@
     pltpu.make_async_copy(xn, xn, local_sem.at[2]).wait()
 
     def fill(k):
-        row = g_rows[0, k, 0]
+        row = g_rows[0, k]
         xb[k, :tok] = xn[row]
         xb[k, tok:] = xs[row]
 
-    loop(n, fill)
+    each(n, fill)
     hid[n] = jnp.zeros((2 * tok, blk), BF16)
-
-    def project(j, first):
+    gate[n] = jnp.zeros((2 * tok, blk), F32)
+    up[n] = jnp.zeros((2 * tok, blk), F32)
+    dh[n] = jnp.zeros((tok, blk), F32)
+    y_sum[n] = jnp.zeros((tok, blk), F32)
+    dx_sum[n] = jnp.zeros((tok, blk), F32)
+
+    gu_order = [me, partner] + peers + [c * 2 + 1 - core for c in peer_chips]
+    gu_keys = [g_cols[0, o] for o in gu_order]
+    dn_keys = [d_rows[0, o] for o in order]
+    g_keys = [g_cols[0, k] for k in range(n)]
+
+    def project(p):
+        j = gu_order[p]
         live = (g_live[0, j] > 0).astype(F32)
-        for g, acc in ((0, gate), (1, up)):
-            part = (dot(xb[j], gu_all[j, g], 1, 0) * live).astype(BF16).astype(F32)
-
-            def add(k):
-                same = (g_cols[0, j, 0] == g_cols[0, k, 0]).astype(F32)
-                if first:
-                    acc[k] = part * same
-                else:
-                    acc[k] = acc[k] + part * same
-
-            loop(n, add)
+        tiles = jnp.concatenate([gu_all[j, 0], gu_all[j, 1]], axis=1)
+        part = (dot(xb[j], tiles, 1, 0) * live).astype(BF16).astype(F32)
+        before = latest(gu_keys, gu_keys[p], p, n)
+        gate[p] = part[:, :blk] + gate[before]
+        up[p] = part[:, blk:] + up[before]
 
     def gu_arrival(o):
         remote(gu_ref, gu_all.at[o], gu_send.at[0], gu_recv.at[o], tile=partner).wait_recv()
@@ -179,9 +207,11 @@
     def dn_arrival(o):
         remote(dn_ref, dn_all.at[o], dn_send.at[0], dn_recv.at[o], tile=partner).wait_recv()
 
-    project(me, True)
+    for copy in own_tiles:
+        copy.wait()
+    project(0)
     gu_arrival(partner)
-    project(partner, False)
+    project(1)
     for i, peer in enumerate(peers):
         gu_arrival(peer)
         start(
@@ -190,7 +220,7 @@
                 tile=partner,
             )
         )
-        project(peer, False)
+        project(2 + i)
     for i, peer in enumerate(peers):
         dn_arrival(peer)
         start(
@@ -199,47 +229,39 @@
                 tile=partner,
             )
         )
-    for c in peer_chips:
-        other = c * 2 + 1 - core
-        gu_arrival(other)
-        project(other, False)
+    for i, c in enumerate(peer_chips):
+        gu_arrival(c * 2 + 1 - core)
+        project(2 + len(peers) + i)
 
     def activate(k):
-        gn = gate[k, :tok]
-        hid[k, :tok] = (gn * jax.nn.sigmoid(gn) * up[k, :tok]).astype(BF16)
-        g = gate[k, tok:]
-        u = up[k, tok:]
+        at = latest(gu_keys, g_cols[0, k], n, n)
+        g = gate[at]
+        u = up[at]
         sig = jax.nn.sigmoid(g)
         act = g * sig
-        hid[k, tok:] = (act * u).astype(BF16)
-        gate[k, tok:] = u * sig * (1.0 + g * (1.0 - sig))
-        up[k, tok:] = act
-
-    loop(n, activate)
+        hid[k] = (act * u).astype(BF16)
+        g, u, sig, act = g[tok:], u[tok:], sig[tok:], act[tok:]
+        slope[k, 0] = u * sig * (1.0 + g * (1.0 - sig))
+        slope[k, 1] = act
+
+    each(n, activate)
 
     def hidden_slot(j):
-        found = jnp.int32(n)
-        for k in range(n):
-            back = n - 1 - k
-            same = (g_cols[0, back, 0] == d_rows[0, j, 0]).astype(I32)
-            found = found + same * (back - found)
-        return found
+        return latest(g_keys, d_rows[0, j], n, n)
 
     dn_arrival(partner)
     for c in peer_chips:
         dn_arrival(c * 2 + 1 - core)
 
-    def forward(j):
+    y_keys = [d_cols[0, k] for k in range(n)]
+    dx_keys = [g_rows[0, k] for k in range(n)]
+
+    for j in range(n):
         live = (d_live[0, j] > 0).astype(F32)
-        h = hid[hidden_slot(j), :tok]
-        y_ref[j] = (dot(h, dn_all[j], 1, 0) * live).astype(BF16)
-
-    loop(n, forward)
-
-    def zero(k):
-        dh[k] = jnp.zeros((tok, blk), F32)
-
-    loop(n, zero)
+        part = (dot(hid[hidden_slot(j), :tok], dn_all[j], 1, 0) * live).astype(BF16)
+        total = part.astype(F32) + y_sum[latest(y_keys, y_keys[j], j, n)]
+        y_sum[j] = total
+        y_ref[j] = total.astype(BF16)
 
     for at, slot in enumerate(order):
         c = at % chips
@@ -250,11 +272,7 @@
         dy = cot[slot]
         part = (dot(dy, dn_all[slot], 1, 1) * live).astype(BF16).astype(F32)
 
-        def add(k):
-            same = (d_rows[0, slot, 0] == g_cols[0, k, 0]).astype(F32)
-            dh[k] = dh[k] + part * same
-
-        loop(n, add)
+        dh[at] = part + dh[latest(dn_keys, dn_keys[at], at, n)]
         term = dot(hid[hidden_slot(slot), tok:], dy, 0, 0) * live
         if at < chips:
             dn_give[c] = term.astype(BF16)
@@ -268,20 +286,20 @@
             dn_own[c] = term
 
     def grads(k):
-        d = dh[k]
-        dg[k, 0] = (d * gate[k, tok:]).astype(BF16)
-        dg[k, 1] = (d * up[k, tok:]).astype(BF16)
-
-    loop(n, grads)
-
-    def gu_term(slot, g):
+        d = dh[latest(dn_keys, g_cols[0, k], n, n)]
+        dg[k] = jnp.concatenate(
+            [(d * slope[k, 0]).astype(BF16), (d * slope[k, 1]).astype(BF16)], axis=1
+        )
+
+    each(n, grads)
+
+    def gu_term(slot):
         live = (g_live[0, slot] > 0).astype(F32)
-        return dot(xb[slot, tok:], dg[slot, g], 0, 0) * live
+        return dot(xb[slot, tok:], dg[slot], 0, 0) * live
 
     for c in range(chips):
         slot = 2 * c + 1 - core
-        for g in range(2):
-            gu_give[c, g] = gu_term(slot, g).astype(BF16)
+        gu_give[c] = gu_term(slot).astype(BF16)
         start(
             remote(
                 gu_give.at[c], gu_got.at[c], half_send.at[1, c], half_recv.at[1, c], tile=partner
@@ -303,12 +321,10 @@
             )
         )
     for c in range(chips):
-        for g in range(2):
-            gu_own[c, g] = gu_term(2 * c + core, g)
+        gu_own[c] = gu_term(2 * c + core)
     for i, c in enumerate(peer_chips):
         half_arrival(1, gu_give, gu_got, c)
-        for g in range(2):
-            gu_out[i, g] = (gu_own[c, g] + gu_got[c, g].astype(F32)).astype(BF16)
+        gu_out[i] = (gu_own[c] + gu_got[c].astype(F32)).astype(BF16)
         start(
             remote(
                 gu_out.at[i], gu_in.at[chip], full_send.at[1, i], full_recv.at[1, chip],
@@ -316,12 +332,13 @@
             )
         )
 
-    def backward(k):
+    for k in range(n):
         live = (g_live[0, k] > 0).astype(F32)
-        both = dot(dg[k, 0], gu_all[k, 0], 1, 1) + dot(dg[k, 1], gu_all[k, 1], 1, 1)
-        dx_ref[k] = (both * live).astype(BF16)
-
-    loop(n, backward)
+        tiles = jnp.concatenate([gu_all[k, 0], gu_all[k, 1]], axis=1)
+        part = (dot(dg[k], tiles, 1, 1) * live).astype(BF16)
+        total = part.astype(F32) + dx_sum[latest(dx_keys, dx_keys[k], k, n)]
+        dx_sum[k] = total
+        dx_ref[k] = total.astype(BF16)
 
     half_arrival(0, dn_give, dn_got, chip)
     half_arrival(1, gu_give, gu_got, chip)
@@ -336,39 +353,60 @@
         remote(
             gu_out.at[0], gu_in.at[c], full_send.at[1, 0], full_recv.at[1, c], tile=partner
         ).wait_recv()
-    for g in range(2):
-        total = gu_own[chip, g] + gu_got[chip, g].astype(F32)
-        for c in peer_chips:
-            total = total + gu_in[c, g].astype(F32)
-        ggu_ref[g] = total
+    total = gu_own[chip] + gu_got[chip].astype(F32)
+    for c in peer_chips:
+        total = total + gu_in[c].astype(F32)
+    ggu_ref[0] = total[:, :blk]
+    ggu_ref[1] = total[:, blk:]
     idx_copy.wait_send()
     for copy in sends:
         copy.wait_send()
 
 
-def place_kernel(n, d_cols, g_rows, y_part, dx_part, y_hbm, dx_hbm, y_buf, dx_buf, sem):
-    tok, blk = y_part.shape[1:]
-    copies = []
-    for at, (index, part, buf, hbm) in enumerate(
-        ((d_cols, y_part, y_buf, y_hbm), (g_rows, dx_part, dx_buf, dx_hbm))
-    ):
+def place_kernel(
+    n,
+    d_cols,
+    g_rows,
+    y_part,
+    dx_part,
+    ggu,
+    gdn,
+    y_hbm,
+    dx_hbm,
+    ggu_hbm,
+    gdn_hbm,
+    y_buf,
+    dx_buf,
+    y_in,
+    dx_in,
+    ggu_in,
+    gdn_in,
+    in_sem,
+    out_sem,
+):
+    blk = y_part.shape[-1]
+    pairs = ((y_part, y_in), (dx_part, dx_in), (ggu, ggu_in), (gdn, gdn_in))
+    reads = [pltpu.make_async_copy(a, b, in_sem.at[i]) for i, (a, b) in enumerate(pairs)]
+    pairs = ((y_buf, y_hbm), (dx_buf, dx_hbm), (ggu_in, ggu_hbm), (gdn_in, gdn_hbm))
+    writes = [pltpu.make_async_copy(a, b, out_sem.at[i]) for i, (a, b) in enumerate(pairs)]
+    for read in reads:
+        read.start()
+
+    for at, (index, part, buf) in enumerate(((d_cols, y_in, y_buf), (g_rows, dx_in, dx_buf))):
         buf[...] = jnp.zeros_like(buf)
+        reads[at].wait()
 
         def put(j):
-            def add(k, total):
-                same = (index[0, k, 0] == index[0, j, 0]).astype(F32)
-                return total + part[k].astype(F32) * same
-
-            total = lax.fori_loop(0, n, add, jnp.zeros((tok, blk), F32))
-            col = pl.multiple_of(index[0, j, 0] * blk, blk)
-            buf[:, pl.ds(col, blk)] = total.astype(BF16)
-
-        loop(n, put)
-        copy = pltpu.make_async_copy(buf, hbm, sem.at[at])
-        copy.start()
-        copies.append(copy)
-    for copy in copies:
-        copy.wait()
+            col = pl.multiple_of(index[0, j] * blk, blk)
+            buf[:, pl.ds(col, blk)] = part[j]
+
+        each(n, put)
+        writes[at].start()
+    for at in (2, 3):
+        reads[at].wait()
+        writes[at].start()
+    for write in writes:
+        write.wait()
 
 
 def per_device(
@@ -405,34 +443,37 @@
             jax.ShapeDtypeStruct((2, blk, blk), F32),
             jax.ShapeDtypeStruct((blk, blk), F32),
         ),
-        in_specs=[smem] * 6 + [vmem] * 2 + [hbm] * 3,
+        in_specs=[smem] * 6 + [pl.BlockSpec(memory_space=pltpu.HBM)] * 5,
         out_specs=(vmem, vmem, vmem, vmem),
         scratch_shapes=[
             pltpu.VMEM((width // blk, tok, blk), BF16),
             pltpu.VMEM((width // blk, tok, blk), BF16),
             pltpu.VMEM((width // blk, tok, blk), BF16),
-            pltpu.SMEM((1, n, 1), I32),
+            pltpu.SMEM((1, n), I32),
             pltpu.VMEM((n, 2, blk, blk), BF16),
             pltpu.VMEM((n, blk, blk), BF16),
             pltpu.VMEM((n, tok, blk), BF16),
             pltpu.VMEM((n, tok, blk), BF16),
             pltpu.VMEM((n, 2 * tok, blk), BF16),
-            pltpu.VMEM((n, 2 * tok, blk), F32),
-            pltpu.VMEM((n, 2 * tok, blk), F32),
+            pltpu.VMEM((n + 1, 2 * tok, blk), F32),
+            pltpu.VMEM((n + 1, 2 * tok, blk), F32),
+            pltpu.VMEM((n, 2, tok, blk), F32),
             pltpu.VMEM((n + 1, 2 * tok, blk), BF16),
-            pltpu.VMEM((n, tok, blk), F32),
-            pltpu.VMEM((n, 2, tok, blk), BF16),
-            pltpu.VMEM((chips, 2, blk, blk), BF16),
-            pltpu.VMEM((chips, 2, blk, blk), BF16),
-            pltpu.VMEM((chips, 2, blk, blk), F32),
-            pltpu.VMEM((chips, 2, blk, blk), BF16),
-            pltpu.VMEM((chips, 2, blk, blk), BF16),
+            pltpu.VMEM((n + 1, tok, blk), F32),
+            pltpu.VMEM((n + 1, tok, blk), F32),
+            pltpu.VMEM((n + 1, tok, blk), F32),
+            pltpu.VMEM((n, tok, 2 * blk), BF16),
+            pltpu.VMEM((chips, blk, 2 * blk), BF16),
+            pltpu.VMEM((chips, blk, 2 * blk), BF16),
+            pltpu.VMEM((chips, blk, 2 * blk), F32),
+            pltpu.VMEM((chips, blk, 2 * blk), BF16),
+            pltpu.VMEM((chips, blk, 2 * blk), BF16),
             pltpu.VMEM((chips, blk, blk), BF16),
             pltpu.VMEM((chips, blk, blk), BF16),
             pltpu.VMEM((chips, blk, blk), F32),
             pltpu.VMEM((chips, blk, blk), BF16),
             pltpu.VMEM((chips, blk, blk), BF16),
-            dma((3,)),
+            dma((5,)),
             dma((2,)),
             dma((2 * chips,)),
             dma((n,)),
@@ -446,14 +487,14 @@
             dma((2, chips)),
         ],
         compiler_params=pltpu.CompilerParams(
-            collective_id=0, has_side_effects=True, vmem_limit_bytes=60 * 1024 * 1024
+            collective_id=0, has_side_effects=True, vmem_limit_bytes=62 << 20
         ),
     )(
-        gu_rows,
-        gu_cols,
+        gu_rows.reshape(1, n),
+        gu_cols.reshape(1, n),
         gu_live,
-        down_rows,
-        down_cols,
+        down_rows.reshape(1, n),
+        down_cols.reshape(1, n),
         down_live,
         gate_up_tiles.reshape(2, blk, blk),
         down_tiles.reshape(blk, blk),
@@ -461,22 +502,29 @@
         x_saved.reshape(tok, width),
         pending.reshape(tok, width),
     )
-    y, dx = pl.pallas_call(
+    y, dx, ggu, gdn = pl.pallas_call(
         functools.partial(place_kernel, n),
         name="place",
         out_shape=(
             jax.ShapeDtypeStruct((tok, width), BF16),
             jax.ShapeDtypeStruct((tok, width), BF16),
+            jax.ShapeDtypeStruct((2, blk, blk), F32),
+            jax.ShapeDtypeStruct((blk, blk), F32),
         ),
-        in_specs=[smem] * 2 + [vmem] * 2,
-        out_specs=(hbm, hbm),
+        in_specs=[smem] * 2 + [hbm] * 4,
+        out_specs=(hbm,) * 4,
         scratch_shapes=[
             pltpu.VMEM((tok, width), BF16),
             pltpu.VMEM((tok, width), BF16),
-            dma((2,)),
+            pltpu.VMEM((n, tok, blk), BF16),
+            pltpu.VMEM((n, tok, blk), BF16),
+            pltpu.VMEM((2, blk, blk), F32),
+            pltpu.VMEM((blk, blk), F32),
+            dma((4,)),
+            dma((4,)),
         ],
-        compiler_params=pltpu.CompilerParams(vmem_limit_bytes=32 * 1024 * 1024),
-    )(down_cols, gu_rows, y_part, dx_part)
+        compiler_params=pltpu.CompilerParams(vmem_limit_bytes=62 << 20),
+    )(down_cols.reshape(1, n), gu_rows.reshape(1, n), y_part, dx_part, ggu, gdn)
     return (
         y[None],
         dx[None],

time: 45.3 us -> 29.4 us (0.65)
  local copies, waits for them, and re-layouts: 10.2 us -> 0 us
  Pallas kernels: 33.9 us -> 28.5 us
    unnamed x14 -> x0, local copies, waits for them, and re-layouts: 10.2 us -> none
    pallas_call x1, Pallas kernels: 29.7 us -> 24.6 us  [per_device(): pl.pallas_call(functools.partial(relay_kernel, n, pipes, side), name='rel...]
where the time goes in v2:
time: 29.4 us; the launch traced here: 29.2 us
  Pallas kernels  28.5 us (97%)
  between operations  0.64 us (2%)
    pallas_call x1, Pallas kernels, per_device(): pl.pallas_call(functools.partial(relay_kernel, n, pipes, side), name='rel...  24.6 us
    pallas_call x1, Pallas kernels, per_device(): pl.pallas_call(functools.partial(place_kernel, n), name='place', out_shap...  3.93 us

profile of v2, /device:TPU:0, one launch (start us, length us, event | category | flops | bytes accessed | tf_op | source)
XLA Modules:
  0.0 29.2 jit_solution(11331191461183028392)
XLA Ops:
  0.6 24.6 %relay.1 = (bf16[8,128,128]{2,1,0:T(8,128)(2,1)}, bf16[8,128,128]{2,1,0:T(8,128)(2,1)}, f32[2,128,128]{2,1,0:T(8,128)}, f32[128,128]{1,0:T(8,128)}) custom-call(s32[1,8]{1,0:T(1,128)} %bitcast.20, s32[1,8]{1,0:T(1,128)} %bitcast.22, s32[1,8]{1,0:T(1,128)} %g_live.1, s32[1,8]{1,0:T(1,128)} %bitcast.23, s32[1,8]{1,0:T(1,128)} %bitcast.18, s32[1,8]{1,0:T(1,128)} %d_live.1, ...), custom_call_target="tpu_custom_call" | custom-call | tf_op jit(solution)/shard_map/relay/pallas_call | solution.py:437
  25.2 3.9 %place.1 = (bf16[128,8192]{1,0:T(8,128)(2,1)}, bf16[128,8192]{1,0:T(8,128)(2,1)}, f32[2,128,128]{2,1,0:T(8,128)}, f32[128,128]{1,0:T(8,128)}) custom-call(s32[1,8]{1,0:T(1,128)} %bitcast.19, s32[1,8]{1,0:T(1,128)} %bitcast.21, bf16[8,128,128]{2,1,0:T(8,128)(2,1)} %get-tuple-element.12.y_part, bf16[8,128,128]{2,1,0:T(8,128)(2,1)} %get-tuple-element.13.dx_part, ...), custom_call_target="tpu_custom_call" | custom-call | tf_op jit(solution)/shard_map/place/pallas_call | solution.py:505

commit v3 on v2

--- a/solution.py
+++ b/solution.py
@@ -124,11 +124,9 @@
         )
 
     def fetch(hbm, buf, at):
-        def piece(b):
-            cols = pl.ds(pl.multiple_of(b * blk, blk), blk)
+        for b in range(buf.shape[0]):
+            cols = pl.ds(b * blk, blk)
             pltpu.make_async_copy(hbm.at[:, cols], buf.at[b], local_sem.at[at]).start()
-
-        loop(buf.shape[0], piece)
 
     barrier = pltpu.get_barrier_semaphore()
     for where in (nxt, prv):
@@ -297,7 +295,7 @@
         live = (g_live[0, slot] > 0).astype(F32)
         return dot(xb[slot, tok:], dg[slot], 0, 0) * live
 
-    for c in range(chips):
+    for c in peer_chips + [chip]:
         slot = 2 * c + 1 - core
         gu_give[c] = gu_term(slot).astype(BF16)
         start(
@@ -320,7 +318,7 @@
                 tile=2 * c + core,
             )
         )
-    for c in range(chips):
+    for c in peer_chips + [chip]:
         gu_own[c] = gu_term(2 * c + core)
     for i, c in enumerate(peer_chips):
         half_arrival(1, gu_give, gu_got, c)

time: 29.4 us -> 29.3 us (level)
  no operation moved by 1% of the time
where the time goes in v3:
time: 29.3 us; the launch traced here: 29.1 us
  Pallas kernels  28.5 us (97%)
  between operations  0.64 us (2%)
    pallas_call x1, Pallas kernels, per_device(): pl.pallas_call(functools.partial(relay_kernel, n, pipes, side), name='rel...  24.6 us
    pallas_call x1, Pallas kernels, per_device(): pl.pallas_call(functools.partial(place_kernel, n), name='place', out_shap...  3.93 us

profile of v3, /device:TPU:0, one launch (start us, length us, event | category | flops | bytes accessed | tf_op | source)
XLA Modules:
  0.0 29.1 jit_solution(2787917438466258618)
XLA Ops:
  0.6 24.6 %relay.1 = (bf16[8,128,128]{2,1,0:T(8,128)(2,1)}, bf16[8,128,128]{2,1,0:T(8,128)(2,1)}, f32[2,128,128]{2,1,0:T(8,128)}, f32[128,128]{1,0:T(8,128)}) custom-call(s32[1,8]{1,0:T(1,128)} %bitcast.20, s32[1,8]{1,0:T(1,128)} %bitcast.22, s32[1,8]{1,0:T(1,128)} %g_live.1, s32[1,8]{1,0:T(1,128)} %bitcast.23, s32[1,8]{1,0:T(1,128)} %bitcast.18, s32[1,8]{1,0:T(1,128)} %d_live.1, ...), custom_call_target="tpu_custom_call" | custom-call | tf_op jit(solution)/shard_map/relay/pallas_call | solution.py:435
  25.2 3.9 %place.1 = (bf16[128,8192]{1,0:T(8,128)(2,1)}, bf16[128,8192]{1,0:T(8,128)(2,1)}, f32[2,128,128]{2,1,0:T(8,128)}, f32[128,128]{1,0:T(8,128)}) custom-call(s32[1,8]{1,0:T(1,128)} %bitcast.19, s32[1,8]{1,0:T(1,128)} %bitcast.21, bf16[8,128,128]{2,1,0:T(8,128)(2,1)} %get-tuple-element.12.y_part, bf16[8,128,128]{2,1,0:T(8,128)(2,1)} %get-tuple-element.13.dx_part, ...), custom_call_target="tpu_custom_call" | custom-call | tf_op jit(solution)/shard_map/place/pallas_call | solution.py:503
